TPU v7x, 32 devices: a whole 2x2x4 slice. The times are simulated.
32 devices in a mesh: groups: 2 (over y), tm: 4 (over z), space: 2 (over x), chan: 2 (over core).
Axes of the slice: x: 2, y: 2, z: 4, core: 2. Of those that a mesh axis runs over, the one named last changes fastest.
Arguments:
- latents: bfloat16 [8, 8, 160, 384], P(('groups', 'tm'), 'space', None, 'chan'), parts along dimension 0, may hold values from -30 to 30
- norm_gain: float32 [384], P('chan'), may hold values from 0.1 to 1.9
- conv_weight: bfloat16 [3, 3, 3, 384, 384], P(None, None, None, 'chan'), may hold values from -0.0625 to 0.0625
- conv_bias: float32 [384], P('chan'), may hold values from -2 to 2
- attention_gain: float32 [384], P('chan'), may hold values from 0.1 to 1.9
- qkv_weight: bfloat16 [384, 1152], P('chan'), may hold values from -3 to 3
- out_weight: bfloat16 [384, 384], replicated, may hold values from -0.3125 to 0.3125
Outputs:
- block_output: bfloat16 [8, 8, 160, 384], P(('groups', 'tm'), 'space', None, 'chan'), parts along dimension 0
There are 2 independent parts, one for each index of `groups`. A program takes and returns all parts, laid end to end along the dimension named above; an argument that names none is the same for every part. Nothing has to cross between parts.
All inputs are finite; a program needn't handle non-finite values.
Results may differ from a plain program's by a relative error of at most 0.019.
Values may be sent and summed in bfloat16 or wider, within the bound.
No kernel may reach another device: no remote copies, remote signals or barrier semaphores. Data moves between devices by JAX's collectives and lax.ppermute only.
A program may use at most 64 MiB of HBM per device.

v0:
```python
import math
import jax
import jax.numpy as jnp
from jax import lax
from jax.sharding import PartitionSpec as P

epsilon = 1e-06


def passed_along(shard, axis, by):
    peers = lax.axis_size(axis)
    pairs = [(i, i + by) for i in range(peers) if 0 <= i + by < peers]
    return lax.ppermute(shard, axis, pairs)


def extended(cells, sides, width):
    for axis, dim in sides:
        count = lax.axis_size(axis)
        ends = count - 1
        head = lax.slice_in_dim(cells, 0, width, axis=dim)
        tail = lax.slice_in_dim(cells, cells.shape[dim] - width, cells.shape[dim], axis=dim)
        cells = jnp.concatenate(
            [
                lax.ppermute(tail, axis, [(i, (i + 1) % count) for i in range(ends)]),
                cells,
                lax.ppermute(head, axis, [((i + 1) % count, i) for i in range(ends)]),
            ],
            axis=dim,
        )
    return cells


def attend_update(running, queries, key_rows, value_rows, score_scale):
    peak, total, summed = running
    scores = (
        lax.dot_general(
            queries, key_rows, (((1,), (1,)), ((), ())), preferred_element_type=jnp.float32
        )
        * score_scale
    )
    new_peak = jnp.maximum(peak, jnp.max(scores, axis=1))
    weights = jnp.exp(scores - new_peak[:, None])
    total = jnp.sum(weights, axis=1)
    summed = jnp.dot(weights.astype(jnp.bfloat16), value_rows, preferred_element_type=jnp.float32)
    return (new_peak, total, summed)


def shards(latents, norm_gain, conv_weight, conv_bias, attention_gain, qkv_weight, out_weight):
    row_count = latents.shape[1]
    col_count = latents.shape[2]
    half_chan = latents.shape[3]
    channels = conv_weight.shape[4]
    pos_count = row_count * col_count
    core_count = lax.axis_size("chan")
    own_rows = pos_count // core_count
    score_scale = 1.0 / math.sqrt(channels)
    input_float = latents[0].astype(jnp.float32)
    square_sums = lax.psum(jnp.sum(input_float * input_float, axis=-1), "chan")
    first = jax.nn.silu(
        input_float * lax.rsqrt(square_sums / channels + epsilon)[..., None] * norm_gain
    ).astype(jnp.bfloat16)
    previous = passed_along(first, "tm", 1)
    earlier = passed_along(first, "tm", 2)
    stacked = jnp.stack([earlier, previous, first])
    rimmed = extended(stacked, (("space", 1),), 1)
    padded = jnp.pad(rimmed, ((0, 0), (0, 0), (1, 1), (0, 0)))
    pieces = []
    for frame_off in range(3):
        for row_off in range(3):
            for col_off in range(3):
                pieces.append(
                    padded[
                        frame_off, row_off : row_off + row_count, col_off : col_off + col_count
                    ].reshape(pos_count, half_chan)
                )
    columns = jnp.concatenate(pieces, axis=1)
    flat_weight = conv_weight.reshape(27 * half_chan, channels)
    partial_value = jnp.dot(columns, flat_weight, preferred_element_type=jnp.float32)
    own_part = lax.psum_scatter(partial_value, "chan", scatter_dimension=1, tiled=True)
    stream_float = (
        (input_float.reshape(pos_count, half_chan) + own_part + conv_bias)
        .astype(jnp.bfloat16)
        .astype(jnp.float32)
    )
    stream_sums = lax.psum(jnp.sum(stream_float * stream_float, axis=-1), "chan")
    second = (
        stream_float * lax.rsqrt(stream_sums / channels + epsilon)[:, None] * attention_gain
    ).astype(jnp.bfloat16)
    initial = (
        jnp.full((own_rows,), -1e30, jnp.float32),
        jnp.zeros((own_rows,), jnp.float32),
        jnp.zeros((own_rows, channels), jnp.float32),
    )
    owned_inputs = lax.all_to_all(second, "chan", split_axis=0, concat_axis=1, tiled=True)
    owned_weights = lax.all_gather(qkv_weight, "chan", axis=0, tiled=True)
    own_qkv = jnp.dot(owned_inputs, owned_weights, preferred_element_type=jnp.float32).astype(
        jnp.bfloat16
    )
    own_queries = own_qkv[:, :channels]
    running = attend_update(
        initial,
        own_queries,
        lax.all_gather(own_qkv[:, channels : 2 * channels], ("space", "chan"), axis=0, tiled=True),
        lax.all_gather(own_qkv[:, 2 * channels :], ("space", "chan"), axis=0, tiled=True),
        score_scale,
    )
    attended = (running[2] / running[1][:, None]).astype(jnp.bfloat16)
    projected = jnp.dot(attended, out_weight, preferred_element_type=jnp.float32).astype(
        jnp.bfloat16
    )
    restored = lax.all_to_all(projected, "chan", split_axis=1, concat_axis=0, tiled=True)
    output = (stream_float + restored.astype(jnp.float32)).astype(jnp.bfloat16)
    return output.reshape(1, row_count, col_count, half_chan)


def solution(mesh):
    placed = (
        P(("groups", "tm"), "space", None, "chan"),
        P("chan"),
        P(None, None, None, "chan", None),
        P("chan"),
        P("chan"),
        P("chan", None),
        P(),
    )
    return jax.shard_map(
        shards,
        mesh=mesh,
        in_specs=placed,
        out_specs=P(("groups", "tm"), "space", None, "chan"),
        check_vma=False,
    )
```

profile of v0, /device:TPU:0, one launch (start us, length us, event | category | flops | bytes accessed | tf_op | source)
XLA Modules:
  0.0 130.4 jit_solution(6493389005145552808)
XLA Ops:
  6.5 1.2 fusion.13
  7.8 2.6 %psum.14 = f32[4,160]{1,0:T(4,128)S(1)} all-reduce(f32[4,160]{1,0:T(4,128)S(1)} %fusion.13), channel_id=1, replica_groups=mesh['groups'=2,'tm'=4,'space'=2,'chan'=2] {'chan'}, use_global_device_ids=true, to_apply=%region_1.0 | all-reduce | flops 640 | bytes 5120 | tf_op jit(solution)/shard_map/psum | solution.py:58
  10.4 1.3 multiply_convert_fusion.1
  11.7 5.8 %collective-permute-start = (bf16[4,160,192]{2,1,0:T(8,128)(2,1)S(1)}, bf16[4,160,192]{2,1,0:T(8,128)(2,1)S(1)}, u32[]{:S(2)}, u32[]{:S(2)}) collective-permute-start(bf16[4,160,192]{2,1,0:T(8,128)(2,1)S(1)} %multiply_convert_fusion.1), channel_id=1, source_target_pairs={{0,8},{4,12},{1,9},{5,13},{2,10},{6,14},{3,11},{7,15},{16,24},{20,... | collective-permute-start | bytes 737288 | tf_op jit(solution)/shard_map/ppermute | solution.py:13
  17.5 3.5 %collective-permute-start.1 = (bf16[4,160,192]{2,1,0:T(8,128)(2,1)S(1)}, bf16[4,160,192]{2,1,0:T(8,128)(2,1)S(1)}, u32[]{:S(2)}, u32[]{:S(2)}) collective-permute-start(bf16[4,160,192]{2,1,0:T(8,128)(2,1)S(1)} %multiply_convert_fusion.1), channel_id=1, source_target_pairs={{0,4},{4,8},{8,12},{1,5},{5,9},{9,13},{2,6},{6,10},{10,14},{3,7},{... | collective-permute-start | bytes 737288 | tf_op jit(solution)/shard_map/ppermute | solution.py:13
  21.0 1.3 multiply_convert_fusion
  22.3 3.3 %collective-permute-done = bf16[4,160,192]{2,1,0:T(8,128)(2,1)S(1)} collective-permute-done((bf16[4,160,192]{2,1,0:T(8,128)(2,1)S(1)}, bf16[4,160,192]{2,1,0:T(8,128)(2,1)S(1)}, u32[]{:S(2)}, u32[]{:S(2)}) %collective-permute-start) | collective-permute-done | bytes 245792 | tf_op jit(solution)/shard_map/ppermute | solution.py:13
  25.6 6.2 %collective-permute-done.1 = bf16[4,160,192]{2,1,0:T(8,128)(2,1)S(1)} collective-permute-done((bf16[4,160,192]{2,1,0:T(8,128)(2,1)S(1)}, bf16[4,160,192]{2,1,0:T(8,128)(2,1)S(1)}, u32[]{:S(2)}, u32[]{:S(2)}) %collective-permute-start.1) | collective-permute-done | bytes 245792 | tf_op jit(solution)/shard_map/ppermute | solution.py:13
  32.0 3.4 %collective-permute-start.2 = (bf16[3,1,160,192]{3,2,1,0:T(8,128)(2,1)S(1)}, bf16[3,1,160,192]{3,2,1,0:T(8,128)(2,1)S(1)}, u32[]{:S(2)}, u32[]{:S(2)}) collective-permute-start(bf16[3,1,160,192]{3,2,1,0:T(8,128)(2,1)S(1)} %get-tuple-element.31), channel_id=1, source_target_pairs={{0,2},{1,3},{4,6},{5,7},{8,10},{9,11},{12,14},{13,15},{16,18},{17,... | collective-permute-start | bytes 552968 | tf_op jit(solution)/shard_map/ppermute | solution.py:24
  35.4 1.3 collective-permute-start.3
  36.7 3.4 %collective-permute-done.2 = bf16[3,1,160,192]{3,2,1,0:T(8,128)(2,1)S(1)} collective-permute-done((bf16[3,1,160,192]{3,2,1,0:T(8,128)(2,1)S(1)}, bf16[3,1,160,192]{3,2,1,0:T(8,128)(2,1)S(1)}, u32[]{:S(2)}, u32[]{:S(2)}) %collective-permute-start.2) | collective-permute-done | bytes 184352 | tf_op jit(solution)/shard_map/ppermute | solution.py:24
  40.0 4.1 %collective-permute-done.3 = bf16[3,1,160,192]{3,2,1,0:T(8,128)(2,1)S(1)} collective-permute-done((bf16[3,1,160,192]{3,2,1,0:T(8,128)(2,1)S(1)}, bf16[3,1,160,192]{3,2,1,0:T(8,128)(2,1)S(1)}, u32[]{:S(2)}, u32[]{:S(2)}) %collective-permute-start.3) | collective-permute-done | bytes 184352 | tf_op jit(solution)/shard_map/ppermute | solution.py:26
  44.2 0.7 select_maximum_fusion
  44.9 2.3 %fusion.21 = (bf16[1,4,160,192]{3,2,1,0:T(8,128)(2,1)S(1)}, bf16[1,4,160,192]{3,2,1,0:T(8,128)(2,1)S(1)}, bf16[1,4,160,192]{3,2,1,0:T(8,128)(2,1)S(1)}, bf16[1,4...) fusion(bf16[3,6,162,192]{3,2,1,0:T(8,128)(2,1)S(1)} %select_max, ...), kind=kLoop, calls=%fused_computation.52 | loop fusion | bytes 8847360 | tf_op jit(solution)/shard_map/slice | solution.py:72
  47.2 1.1 pad_maximum_fusion
  48.3 1.0 pad_maximum_fusion.3
  49.3 11.7 %concatenate.19 = bf16[640,5184]{1,0:T(8,128)(2,1)} concatenate(bf16[640,192]{1,0:T(8,128)(2,1)} %bitcast.88, bf16[640,192]{1,0:T(8,128)(2,1)} %bitcast.93, bf16[640,192]{1,0:T(8,128)(2,1)} %bitcast.87, bf16[640,192]{1,0:T(8,128)(2,1)} %bitcast.86, bf16[640,192]{1,0:T(8,128)(2,1)S(1)} %bitcast.64, bf16[640,192]{1,0:T(8,128)(2,1)} %bitcast.85, bf16[640,192]{1,0:T(8,128)(2,1)} %bitcast.84, ...), dimensions={1} | concatenate | bytes 13271040 | tf_op jit(solution)/shard_map/concatenate | solution.py:76
  61.1 8.4 %fusion.24 = f32[640,384]{0,1:T(8,128)} fusion(bf16[640,5184]{1,0:T(8,128)(2,1)} %concatenate.19, bf16[5184,384]{1,0:T(8,128)(2,1)} %bitcast.97), kind=kOutput, calls=%fused_computation.55 | convolution fusion | flops 2548039680 | bytes 11599872 | tf_op jit(solution)/shard_map/dot_general | solution.py:78
  69.7 0.8 copy-done.3
  70.5 2.4 %all_gather.9 = bf16[384,1152]{1,0:T(8,128)(2,1)S(1)} all-gather(bf16[192,1152]{1,0:T(8,128)(2,1)S(1)} %copy-done.3), channel_id=1, replica_groups=mesh['groups'=2,'tm'=4,'space'=2,'chan'=2] {'chan'}, dimensions={0}, use_global_device_ids=true | all-gather | bytes 1327104 | tf_op jit(solution)/shard_map/all_gather | solution.py:95
  72.9 12.9 %reduce-scatter.2.cloned.1.call-done = f32[640,192]{0,1:T(8,128)} async-done(((f32[640,384]{0,1:T(8,128)}), f32[640,192]{0,1:T(8,128)}) %reduce-scatter.2.cloned.1.call-update) | async-done | bytes 491536 | tf_op jit(solution)/shard_map/reduce_scatter | solution.py:79
  85.9 1.2 fusion.15
  87.0 2.5 %psum.15 = f32[640]{0:T(1024)S(1)} all-reduce(f32[640]{0:T(1024)S(1)} %get-tuple-element.5), channel_id=1, replica_groups=mesh['groups'=2,'tm'=4,'space'=2,'chan'=2] {'chan'}, use_global_device_ids=true, to_apply=%region_4.5 | all-reduce | flops 640 | bytes 5120 | tf_op jit(solution)/shard_map/psum | solution.py:85
  89.9 4.0 %all_to_all.32 = bf16[2,320,192]{1,2,0:T(8,128)(2,1)S(1)} all-to-all(bf16[2,320,192]{1,2,0:T(8,128)(2,1)S(1)} %copy.12), channel_id=1, replica_groups=mesh['groups'=2,'tm'=4,'space'=2,'chan'=2] {'chan'}, dimensions={0} | all-to-all | bytes 491520 | tf_op jit(solution)/shard_map/all_to_all | solution.py:94
  93.9 0.6 convolution_convert_fusion
  94.6 9.9 %all_gather.10 = bf16[1280,384]{1,0:T(8,128)(2,1)S(1)} all-gather(bf16[320,384]{1,0:T(8,128)(2,1)S(1)} %get-tuple-element.33), channel_id=1, replica_groups=mesh['groups'=2,'tm'=4,'space'=2,'chan'=2] {'space','chan'}, dimensions={0}, use_global_device_ids=true | all-gather | bytes 1228800 | tf_op jit(solution)/shard_map/all_gather | solution.py:103
  104.5 0.7 fusion.23
  105.2 10.2 %all_gather.11 = bf16[1280,384]{1,0:T(8,128)(2,1)} all-gather(bf16[320,384]{1,0:T(8,128)(2,1)S(1)} %get-tuple-element.34), channel_id=1, replica_groups=mesh['groups'=2,'tm'=4,'space'=2,'chan'=2] {'space','chan'}, dimensions={0}, use_global_device_ids=true | all-gather | bytes 1228800 | tf_op jit(solution)/shard_map/all_gather | solution.py:104
  115.8 0.8 copy-done.2
  116.6 0.9 convolution_convert_fusion.1
  117.7 4.0 %all_to_all.33 = bf16[320,2,192]{0,2,1:T(8,128)(2,1)S(1)} all-to-all(bf16[320,2,192]{0,2,1:T(8,128)(2,1)S(1)} %bitcast.95), channel_id=1, replica_groups=mesh['groups'=2,'tm'=4,'space'=2,'chan'=2] {'chan'}, dimensions={1} | all-to-all | bytes 491520 | tf_op jit(solution)/shard_map/all_to_all | solution.py:111
  122.6 0.9 copy.15
  (27 shorter events, 2.3 us)
Async XLA Ops:
  6.5 109.3 %copy-start = (bf16[384,384]{1,0:T(8,128)(2,1)S(1)}, bf16[384,384]{1,0:T(8,128)(2,1)}, u32[]{:S(2)}) copy-start(bf16[384,384]{1,0:T(8,128)(2,1)} %param.13) | copy-start | bytes 884740
  6.5 79.3 %reduce-scatter.2.cloned.1.call-start = ((), (), s32[]{:S(2)}) async-start(), calls=%async_computation.3 | async-start | bytes 1474560 | tf_op jit(solution)/shard_map/reduce_scatter | solution.py:79
  11.7 13.9 %collective-permute-start = (bf16[4,160,192]{2,1,0:T(8,128)(2,1)S(1)}, bf16[4,160,192]{2,1,0:T(8,128)(2,1)S(1)}, u32[]{:S(2)}, u32[]{:S(2)}) collective-permute-start(bf16[4,160,192]{2,1,0:T(8,128)(2,1)S(1)} %multiply_convert_fusion.1), channel_id=1, source_target_pairs={{0,8},{4,12},{1,9},{5,13},{2,10},{6,14},{3,11},{7,15},{16,24},{20,... | collective-permute-start | bytes 737288 | tf_op jit(solution)/shard_map/ppermute | solution.py:13
  17.5 14.3 %collective-permute-start.1 = (bf16[4,160,192]{2,1,0:T(8,128)(2,1)S(1)}, bf16[4,160,192]{2,1,0:T(8,128)(2,1)S(1)}, u32[]{:S(2)}, u32[]{:S(2)}) collective-permute-start(bf16[4,160,192]{2,1,0:T(8,128)(2,1)S(1)} %multiply_convert_fusion.1), channel_id=1, source_target_pairs={{0,4},{4,8},{8,12},{1,5},{5,9},{9,13},{2,6},{6,10},{10,14},{3,7},{... | collective-permute-start | bytes 737288 | tf_op jit(solution)/shard_map/ppermute | solution.py:13
  32.0 8.1 %collective-permute-start.2 = (bf16[3,1,160,192]{3,2,1,0:T(8,128)(2,1)S(1)}, bf16[3,1,160,192]{3,2,1,0:T(8,128)(2,1)S(1)}, u32[]{:S(2)}, u32[]{:S(2)}) collective-permute-start(bf16[3,1,160,192]{3,2,1,0:T(8,128)(2,1)S(1)} %get-tuple-element.31), channel_id=1, source_target_pairs={{0,2},{1,3},{4,6},{5,7},{8,10},{9,11},{12,14},{13,15},{16,18},{17,... | collective-permute-start | bytes 552968 | tf_op jit(solution)/shard_map/ppermute | solution.py:24
  35.4 8.8 %collective-permute-start.3 = (bf16[3,1,160,192]{3,2,1,0:T(8,128)(2,1)S(1)}, bf16[3,1,160,192]{3,2,1,0:T(8,128)(2,1)S(1)}, u32[]{:S(2)}, u32[]{:S(2)}) collective-permute-start(bf16[3,1,160,192]{3,2,1,0:T(8,128)(2,1)S(1)} %get-tuple-element.32), channel_id=1, source_target_pairs={{2,0},{3,1},{6,4},{7,5},{10,8},{11,9},{14,12},{15,13},{18,16},{19,... | collective-permute-start | bytes 552968 | tf_op jit(solution)/shard_map/ppermute | solution.py:26
  61.1 8.5 %copy-start.1 = (bf16[1,4,160,192]{3,2,1,0:T(8,128)(2,1)S(1)}, bf16[1,4,160,192]{3,2,1,0:T(8,128)(2,1)}, u32[]{:S(2)}) copy-start(bf16[1,4,160,192]{3,2,1,0:T(8,128)(2,1)} %param.7) | copy-start | bytes 737284
  69.5 1.0 copy-start.3
  69.5 16.4 %copy-start.5 = (f32[192]{0:T(256)S(1)}, f32[192]{0:T(256)}, u32[]{:S(2)}) copy-start(f32[192]{0:T(256)} %param.10) | copy-start | bytes 2308
  69.5 20.0 %copy-start.4 = (f32[192]{0:T(256)S(1)}, f32[192]{0:T(256)}, u32[]{:S(2)}) copy-start(f32[192]{0:T(256)} %param.11) | copy-start | bytes 2308
  115.4 1.2 copy-start.2
Sparse Core Ops, SparseCore 0:
  69.7 16.1 reduce-scatter.1
where the time goes:
time: 132 us; the launch traced here: 130 us
  blocking collectives  35.6 us (27%)
  waiting for transfers between devices  30 us (23%)
  local copies, waits for them, and re-layouts  18.1 us (14%)
  starting transfers between devices  14 us (11%)
  between operations  13.6 us (10%)
  matrix products  10.6 us (8%)
  other arithmetic  8.47 us (6%)
    reduce_scatter x1, waiting for transfers between devices, shards(): lax.psum_scatter(partial_value, 'chan', scatter_dimension=1, tiled=True)  12.9 us
    concatenate x1, local copies, waits for them, and re-layouts, shards(): columns = jnp.concatenate(pieces, axis=1)  11.7 us
    all_gather x1, blocking collectives, shards(): lax.all_gather(own_qkv[:, 2 * channels:], ('space', 'chan'), axis=0, tile...  10.2 us
    all_gather x1, blocking collectives, shards(): lax.all_gather(own_qkv[:, channels:2 * channels], ('space', 'chan'), axis...  9.93 us
    ppermute x2, waiting for transfers between devices, passed_along(): return lax.ppermute(shard, axis, pairs)  9.56 us
    ppermute x2, starting transfers between devices, passed_along(): return lax.ppermute(shard, axis, pairs)  9.33 us
    dot_general x1, matrix products, shards(): jnp.dot(columns, flat_weight, preferred_element_type=jnp.float32)  8.42 us
    ppermute x1, waiting for transfers between devices, extended(): lax.ppermute(head, axis, [((i + 1) % count, i) for i in range(ends)])  4.13 us
  transfers between devices with their start and end apart: 5, of which 5 were waited for; matrix products, arithmetic and copies ran while one was open for 1% of the time, Pallas kernels for 0%

commit v1 on v0

--- a/solution.py
+++ b/solution.py
@@ -101,7 +101,15 @@
         initial,
         own_queries,
         lax.all_gather(own_qkv[:, channels : 2 * channels], ("space", "chan"), axis=0, tiled=True),
-        lax.all_gather(own_qkv[:, 2 * channels :], ("space", "chan"), axis=0, tiled=True),
+        jnp.concatenate(
+            lax.all_to_all(
+                jnp.stack([own_qkv[:, 2 * channels :]] * lax.axis_size(("space", "chan"))),
+                ("space", "chan"),
+                0,
+                0,
+            ),
+            axis=0,
+        ),
         score_scale,
     )
     attended = (running[2] / running[1][:, None]).astype(jnp.bfloat16)

time: 132 us -> 139 us (1.053)
  starting transfers between devices: 14 us -> 18.3 us
  matrix products: 10.6 us -> 12.7 us
    all_gather x1 -> x0, blocking collectives: 10.2 us -> none  [shards(): lax.all_gather(own_qkv[:, 2 * channels:], ('space', 'chan'), axis=0, tile...]
    all_gather x1, blocking collectives: 9.93 us -> 19.9 us  [shards(): lax.all_gather(own_qkv[:, channels:2 * channels], ('space', 'chan'), axis...]
    all_to_all x0 -> x1, starting transfers between devices: none -> 4.22 us  [shards(): lax.all_to_all(jnp.stack([own_qkv[:, 2 * channels:]] * lax.axis_size(('sp...]
  transfers between devices with their start and end apart: 5 -> 6, of which waited for: 5 -> 5; matrix products, arithmetic and copies ran while one was open for 1% -> 3% of each run, Pallas kernels for 0% -> 0%
where the time goes in v1:
time: 139 us; the launch traced here: 138 us
  blocking collectives  35.3 us (25%)
  waiting for transfers between devices  30 us (22%)
  local copies, waits for them, and re-layouts  19.3 us (14%)
  starting transfers between devices  18.3 us (13%)
  between operations  13.6 us (10%)
  matrix products  12.7 us (9%)
  other arithmetic  8.46 us (6%)
    all_gather x1, blocking collectives, shards(): lax.all_gather(own_qkv[:, channels:2 * channels], ('space', 'chan'), axis...  19.9 us
    reduce_scatter x1, waiting for transfers between devices, shards(): lax.psum_scatter(partial_value, 'chan', scatter_dimension=1, tiled=True)  12.9 us
    concatenate x1, local copies, waits for them, and re-layouts, shards(): columns = jnp.concatenate(pieces, axis=1)  11.7 us
    ppermute x2, waiting for transfers between devices, passed_along(): return lax.ppermute(shard, axis, pairs)  9.56 us
    ppermute x2, starting transfers between devices, passed_along(): return lax.ppermute(shard, axis, pairs)  9.33 us
    dot_general x1, matrix products, shards(): jnp.dot(columns, flat_weight, preferred_element_type=jnp.float32)  8.41 us
    all_to_all x1, starting transfers between devices, shards(): lax.all_to_all(jnp.stack([own_qkv[:, 2 * channels:]] * lax.axis_size(('sp...  4.22 us
    ppermute x1, waiting for transfers between devices, extended(): lax.ppermute(head, axis, [((i + 1) % count, i) for i in range(ends)])  4.13 us
  transfers between devices with their start and end apart: 6, of which 5 were waited for; matrix products, arithmetic and copies ran while one was open for 3% of the time, Pallas kernels for 0%

profile of v1, /device:TPU:0, one launch (start us, length us, event | category | flops | bytes accessed | tf_op | source)
XLA Modules:
  0.0 137.6 jit_solution(15959119249239768786)
XLA Ops:
  6.5 1.2 fusion.13
  7.8 2.6 %psum.14 = f32[4,160]{1,0:T(4,128)S(1)} all-reduce(f32[4,160]{1,0:T(4,128)S(1)} %fusion.13), channel_id=1, replica_groups=mesh['groups'=2,'tm'=4,'space'=2,'chan'=2] {'chan'}, use_global_device_ids=true, to_apply=%region_1.0 | all-reduce | flops 640 | bytes 5120 | tf_op jit(solution)/shard_map/psum | solution.py:58
  10.4 1.3 multiply_convert_fusion.1
  11.7 5.8 %collective-permute-start = (bf16[4,160,192]{2,1,0:T(8,128)(2,1)S(1)}, bf16[4,160,192]{2,1,0:T(8,128)(2,1)S(1)}, u32[]{:S(2)}, u32[]{:S(2)}) collective-permute-start(bf16[4,160,192]{2,1,0:T(8,128)(2,1)S(1)} %multiply_convert_fusion.1), channel_id=1, source_target_pairs={{0,8},{4,12},{1,9},{5,13},{2,10},{6,14},{3,11},{7,15},{16,24},{20,... | collective-permute-start | bytes 737288 | tf_op jit(solution)/shard_map/ppermute | solution.py:13
  17.5 3.5 %collective-permute-start.1 = (bf16[4,160,192]{2,1,0:T(8,128)(2,1)S(1)}, bf16[4,160,192]{2,1,0:T(8,128)(2,1)S(1)}, u32[]{:S(2)}, u32[]{:S(2)}) collective-permute-start(bf16[4,160,192]{2,1,0:T(8,128)(2,1)S(1)} %multiply_convert_fusion.1), channel_id=1, source_target_pairs={{0,4},{4,8},{8,12},{1,5},{5,9},{9,13},{2,6},{6,10},{10,14},{3,7},{... | collective-permute-start | bytes 737288 | tf_op jit(solution)/shard_map/ppermute | solution.py:13
  21.0 1.3 multiply_convert_fusion
  22.3 3.3 %collective-permute-done = bf16[4,160,192]{2,1,0:T(8,128)(2,1)S(1)} collective-permute-done((bf16[4,160,192]{2,1,0:T(8,128)(2,1)S(1)}, bf16[4,160,192]{2,1,0:T(8,128)(2,1)S(1)}, u32[]{:S(2)}, u32[]{:S(2)}) %collective-permute-start) | collective-permute-done | bytes 245792 | tf_op jit(solution)/shard_map/ppermute | solution.py:13
  25.6 6.2 %collective-permute-done.1 = bf16[4,160,192]{2,1,0:T(8,128)(2,1)S(1)} collective-permute-done((bf16[4,160,192]{2,1,0:T(8,128)(2,1)S(1)}, bf16[4,160,192]{2,1,0:T(8,128)(2,1)S(1)}, u32[]{:S(2)}, u32[]{:S(2)}) %collective-permute-start.1) | collective-permute-done | bytes 245792 | tf_op jit(solution)/shard_map/ppermute | solution.py:13
  32.0 3.4 %collective-permute-start.2 = (bf16[3,1,160,192]{3,2,1,0:T(8,128)(2,1)S(1)}, bf16[3,1,160,192]{3,2,1,0:T(8,128)(2,1)S(1)}, u32[]{:S(2)}, u32[]{:S(2)}) collective-permute-start(bf16[3,1,160,192]{3,2,1,0:T(8,128)(2,1)S(1)} %get-tuple-element.31), channel_id=1, source_target_pairs={{0,2},{1,3},{4,6},{5,7},{8,10},{9,11},{12,14},{13,15},{16,18},{17,... | collective-permute-start | bytes 552968 | tf_op jit(solution)/shard_map/ppermute | solution.py:24
  35.4 1.3 collective-permute-start.3
  36.7 3.4 %collective-permute-done.2 = bf16[3,1,160,192]{3,2,1,0:T(8,128)(2,1)S(1)} collective-permute-done((bf16[3,1,160,192]{3,2,1,0:T(8,128)(2,1)S(1)}, bf16[3,1,160,192]{3,2,1,0:T(8,128)(2,1)S(1)}, u32[]{:S(2)}, u32[]{:S(2)}) %collective-permute-start.2) | collective-permute-done | bytes 184352 | tf_op jit(solution)/shard_map/ppermute | solution.py:24
  40.0 4.1 %collective-permute-done.3 = bf16[3,1,160,192]{3,2,1,0:T(8,128)(2,1)S(1)} collective-permute-done((bf16[3,1,160,192]{3,2,1,0:T(8,128)(2,1)S(1)}, bf16[3,1,160,192]{3,2,1,0:T(8,128)(2,1)S(1)}, u32[]{:S(2)}, u32[]{:S(2)}) %collective-permute-start.3) | collective-permute-done | bytes 184352 | tf_op jit(solution)/shard_map/ppermute | solution.py:26
  44.2 0.7 select_maximum_fusion
  44.9 2.3 %fusion.21 = (bf16[1,4,160,192]{3,2,1,0:T(8,128)(2,1)S(1)}, bf16[1,4,160,192]{3,2,1,0:T(8,128)(2,1)S(1)}, bf16[1,4,160,192]{3,2,1,0:T(8,128)(2,1)S(1)}, bf16[1,4...) fusion(bf16[3,6,162,192]{3,2,1,0:T(8,128)(2,1)S(1)} %select_max, ...), kind=kLoop, calls=%fused_computation.52 | loop fusion | bytes 8847360 | tf_op jit(solution)/shard_map/slice | solution.py:72
  47.3 1.0 pad_maximum_fusion
  48.3 1.0 pad_maximum_fusion.3
  49.3 11.7 %concatenate.19 = bf16[640,5184]{1,0:T(8,128)(2,1)} concatenate(bf16[640,192]{1,0:T(8,128)(2,1)} %bitcast.89, bf16[640,192]{1,0:T(8,128)(2,1)} %bitcast.94, bf16[640,192]{1,0:T(8,128)(2,1)} %bitcast.88, bf16[640,192]{1,0:T(8,128)(2,1)} %bitcast.87, bf16[640,192]{1,0:T(8,128)(2,1)S(1)} %bitcast.65, bf16[640,192]{1,0:T(8,128)(2,1)} %bitcast.86, bf16[640,192]{1,0:T(8,128)(2,1)} %bitcast.85, ...), dimensions={1} | concatenate | bytes 13271040 | tf_op jit(solution)/shard_map/concatenate | solution.py:76
  61.1 8.4 %fusion.24 = f32[640,384]{0,1:T(8,128)} fusion(bf16[640,5184]{1,0:T(8,128)(2,1)} %concatenate.19, bf16[5184,384]{1,0:T(8,128)(2,1)} %bitcast.98), kind=kOutput, calls=%fused_computation.55 | convolution fusion | flops 2548039680 | bytes 11599872 | tf_op jit(solution)/shard_map/dot_general | solution.py:78
  69.7 0.8 copy-done.3
  70.5 2.4 %all_gather.6 = bf16[384,1152]{1,0:T(8,128)(2,1)S(1)} all-gather(bf16[192,1152]{1,0:T(8,128)(2,1)S(1)} %copy-done.3), channel_id=1, replica_groups=mesh['groups'=2,'tm'=4,'space'=2,'chan'=2] {'chan'}, dimensions={0}, use_global_device_ids=true | all-gather | bytes 1327104 | tf_op jit(solution)/shard_map/all_gather | solution.py:95
  72.9 12.9 %reduce-scatter.2.cloned.1.call-done = f32[640,192]{0,1:T(8,128)} async-done(((f32[640,384]{0,1:T(8,128)}), f32[640,192]{0,1:T(8,128)}) %reduce-scatter.2.cloned.1.call-update) | async-done | bytes 491536 | tf_op jit(solution)/shard_map/reduce_scatter | solution.py:79
  85.8 1.2 fusion.15
  87.0 2.5 %psum.15 = f32[640]{0:T(1024)S(1)} all-reduce(f32[640]{0:T(1024)S(1)} %get-tuple-element.5), channel_id=1, replica_groups=mesh['groups'=2,'tm'=4,'space'=2,'chan'=2] {'chan'}, use_global_device_ids=true, to_apply=%region_4.5 | all-reduce | flops 640 | bytes 5120 | tf_op jit(solution)/shard_map/psum | solution.py:85
  89.9 4.0 %all_to_all.37 = bf16[2,320,192]{1,2,0:T(8,128)(2,1)S(1)} all-to-all(bf16[2,320,192]{1,2,0:T(8,128)(2,1)S(1)} %copy.12), channel_id=1, replica_groups=mesh['groups'=2,'tm'=4,'space'=2,'chan'=2] {'chan'}, dimensions={0} | all-to-all | bytes 491520 | tf_op jit(solution)/shard_map/all_to_all | solution.py:94
  94.5 0.9 copy-done.2
  95.4 1.1 stack.20
  96.5 4.2 %all-to-all-start.1 = ((bf16[4,320,384]{2,1,0:T(8,128)(2,1)}), bf16[4,320,384]{2,1,0:T(8,128)(2,1)}, u32[]{:S(2)}, u32[]{:S(2)}) async-start(bf16[4,320,384]{2,1,0:T(8,128)(2,1)} %stack.20), calls=%async_computation.2 | async-start | bytes 1966080 | tf_op jit(solution)/shard_map/all_to_all | solution.py:105
  100.7 19.9 %all_gather.7 = bf16[1280,384]{1,0:T(8,128)(2,1)S(1)} all-gather(bf16[320,384]{1,0:T(8,128)(2,1)S(1)} %get-tuple-element.33), channel_id=1, replica_groups=mesh['groups'=2,'tm'=4,'space'=2,'chan'=2] {'space','chan'}, dimensions={0}, use_global_device_ids=true | all-gather | bytes 1228800 | tf_op jit(solution)/shard_map/all_gather | solution.py:103
  120.5 1.7 %fusion.23 = (f32[320]{0:T(512)S(1)}, f32[320,1280]{1,0:T(8,128)S(1)}) fusion(bf16[1280,384]{1,0:T(8,128)(2,1)S(1)} %all_gather.7, bf16[320,1152]{1,0:T(8,128)(2,1)} %copy-done.2), kind=kOutput, calls=%fused_computation.54 | convolution fusion | flops 315391680 | bytes 2868480 | tf_op jit(solution)/shard_map/dot_general | solution.py:36
  122.6 2.1 %convolution_convert_fusion.1 = bf16[320,384]{1,0:T(8,128)(2,1)S(1)} fusion(bf16[384,384]{1,0:T(8,128)(2,1)S(1)} %copy-done, bf16[1280,384]{1,0:T(8,128)(2,1)} %bitcast.34, f32[320,1280]{1,0:T(8,128)S(1)} %get-tuple-element.36, f32[320]{0:T(512)S(1)} %broadcast_maximum_fusion, f32[320]{0:T(512)S(1)} %fusion.6), kind=kOutput, calls=%fused_computation.17 | convolution fusion | flops 410132480 | bytes 3164672 | tf_op jit(solution)/shard_map/dot_general | solution.py:116
  124.9 4.0 %all_to_all.38 = bf16[320,2,192]{0,2,1:T(8,128)(2,1)S(1)} all-to-all(bf16[320,2,192]{0,2,1:T(8,128)(2,1)S(1)} %bitcast.96), channel_id=1, replica_groups=mesh['groups'=2,'tm'=4,'space'=2,'chan'=2] {'chan'}, dimensions={1} | all-to-all | bytes 491520 | tf_op jit(solution)/shard_map/all_to_all | solution.py:119
  129.8 0.9 copy.15
  (29 shorter events, 2.9 us)
Async XLA Ops:
  6.5 116.1 %copy-start = (bf16[384,384]{1,0:T(8,128)(2,1)S(1)}, bf16[384,384]{1,0:T(8,128)(2,1)}, u32[]{:S(2)}) copy-start(bf16[384,384]{1,0:T(8,128)(2,1)} %param.13) | copy-start | bytes 884740
  6.5 79.3 %reduce-scatter.2.cloned.1.call-start = ((), (), s32[]{:S(2)}) async-start(), calls=%async_computation.4 | async-start | bytes 1474560 | tf_op jit(solution)/shard_map/reduce_scatter | solution.py:79
  11.7 13.9 %collective-permute-start = (bf16[4,160,192]{2,1,0:T(8,128)(2,1)S(1)}, bf16[4,160,192]{2,1,0:T(8,128)(2,1)S(1)}, u32[]{:S(2)}, u32[]{:S(2)}) collective-permute-start(bf16[4,160,192]{2,1,0:T(8,128)(2,1)S(1)} %multiply_convert_fusion.1), channel_id=1, source_target_pairs={{0,8},{4,12},{1,9},{5,13},{2,10},{6,14},{3,11},{7,15},{16,24},{20,... | collective-permute-start | bytes 737288 | tf_op jit(solution)/shard_map/ppermute | solution.py:13
  17.5 14.3 %collective-permute-start.1 = (bf16[4,160,192]{2,1,0:T(8,128)(2,1)S(1)}, bf16[4,160,192]{2,1,0:T(8,128)(2,1)S(1)}, u32[]{:S(2)}, u32[]{:S(2)}) collective-permute-start(bf16[4,160,192]{2,1,0:T(8,128)(2,1)S(1)} %multiply_convert_fusion.1), channel_id=1, source_target_pairs={{0,4},{4,8},{8,12},{1,5},{5,9},{9,13},{2,6},{6,10},{10,14},{3,7},{... | collective-permute-start | bytes 737288 | tf_op jit(solution)/shard_map/ppermute | solution.py:13
  32.0 8.1 %collective-permute-start.2 = (bf16[3,1,160,192]{3,2,1,0:T(8,128)(2,1)S(1)}, bf16[3,1,160,192]{3,2,1,0:T(8,128)(2,1)S(1)}, u32[]{:S(2)}, u32[]{:S(2)}) collective-permute-start(bf16[3,1,160,192]{3,2,1,0:T(8,128)(2,1)S(1)} %get-tuple-element.31), channel_id=1, source_target_pairs={{0,2},{1,3},{4,6},{5,7},{8,10},{9,11},{12,14},{13,15},{16,18},{17,... | collective-permute-start | bytes 552968 | tf_op jit(solution)/shard_map/ppermute | solution.py:24
  35.4 8.8 %collective-permute-start.3 = (bf16[3,1,160,192]{3,2,1,0:T(8,128)(2,1)S(1)}, bf16[3,1,160,192]{3,2,1,0:T(8,128)(2,1)S(1)}, u32[]{:S(2)}, u32[]{:S(2)}) collective-permute-start(bf16[3,1,160,192]{3,2,1,0:T(8,128)(2,1)S(1)} %get-tuple-element.32), channel_id=1, source_target_pairs={{2,0},{3,1},{6,4},{7,5},{10,8},{11,9},{14,12},{15,13},{18,16},{19,... | collective-permute-start | bytes 552968 | tf_op jit(solution)/shard_map/ppermute | solution.py:26
  61.0 8.5 %copy-start.1 = (bf16[1,4,160,192]{3,2,1,0:T(8,128)(2,1)S(1)}, bf16[1,4,160,192]{3,2,1,0:T(8,128)(2,1)}, u32[]{:S(2)}) copy-start(bf16[1,4,160,192]{3,2,1,0:T(8,128)(2,1)} %param.7) | copy-start | bytes 737284
  69.5 1.0 copy-start.3
  69.5 16.4 %copy-start.5 = (f32[192]{0:T(256)S(1)}, f32[192]{0:T(256)}, u32[]{:S(2)}) copy-start(f32[192]{0:T(256)} %param.10) | copy-start | bytes 2308
  69.5 20.0 %copy-start.4 = (f32[192]{0:T(256)S(1)}, f32[192]{0:T(256)}, u32[]{:S(2)}) copy-start(f32[192]{0:T(256)} %param.11) | copy-start | bytes 2308
  94.5 0.9 copy-start.2
  96.5 26.2 %all-to-all-start.1 = ((bf16[4,320,384]{2,1,0:T(8,128)(2,1)}), bf16[4,320,384]{2,1,0:T(8,128)(2,1)}, u32[]{:S(2)}, u32[]{:S(2)}) async-start(bf16[4,320,384]{2,1,0:T(8,128)(2,1)} %stack.20), calls=%async_computation.2 | async-start | bytes 1966080 | tf_op jit(solution)/shard_map/all_to_all | solution.py:105
Sparse Core Ops, SparseCore 0:
  69.6 16.1 reduce-scatter.1
